TPU v7x, 256 devices: a whole 4x4x8 slice. The times are simulated.
256 devices in a mesh: wide: 64 (over z, x, core), narrow: 4 (over y).
Axes of the slice: x: 4, y: 4, z: 8, core: 2. Of those that a mesh axis runs over, the one named last changes fastest.
Arguments:
- coeffs: bfloat16 [2, 1024, 1024, 512], P(None, 'wide', None, 'narrow'), may hold values from -3 to 3
- legendre: bfloat16 [1024, 64, 1024], P('wide'), may hold values from -3 to 3
- order_table: int32 [1024], replicated, may hold values from 0 to 1023, each once
- thresholds: float32 [512], replicated, may hold values from 0.2 to 2
Outputs:
- lowrank: float32 [64, 2048, 512], P('wide', 'narrow')
- sparse: float32 [64, 2048, 512], P('wide', 'narrow')
Inputs may be any that keep to these rules, and one draw needn't show every extreme that they name: `order_table`: each order 0 to 1023 stands in exactly one slot.
All inputs are finite; a program needn't handle non-finite values.
Results may differ from a plain program's by a relative error of at most 0.0003.
Values sent between devices are 32-bit elements; how exact they have to be, the bound alone decides.
A program may use at most 128 MiB of HBM per device.

v0:
```python
import math
import jax
import jax.numpy as jnp
from jax import lax
from jax.sharding import PartitionSpec as P

NPIX = 2048
ITERS = 2


def soft_shrink(values, limits):
    return jnp.sign(values) * jnp.maximum(jnp.abs(values) - limits, 0.0)


def wiener_filter(covariance):
    chan_total = covariance.shape[0]
    ridge_shift = jnp.trace(covariance) / chan_total
    factor = jnp.linalg.cholesky(
        covariance + ridge_shift * jnp.eye(chan_total, dtype=covariance.dtype)
    )
    return jax.scipy.linalg.cho_solve((factor, True), covariance)


def per_device(coeffs, legendre, order_table, thresholds):
    slot_count = legendre.shape[0]
    degrees = legendre.shape[2]
    first_slot = lax.axis_index("wide") * slot_count
    own_orders = lax.dynamic_slice_in_dim(order_table, first_slot, slot_count)
    degree_mask = (
        lax.broadcasted_iota(jnp.int32, (slot_count, degrees), 1) >= own_orders[:, None]
    ).astype(legendre.dtype)
    masked = legendre * degree_mask[:, None, :]
    spectra = jnp.einsum("srl,kslc->ksrc", masked, coeffs, preferred_element_type=jnp.float32)
    pixels = lax.broadcasted_iota(jnp.int32, (1, NPIX), 1)
    pixel_phase = order_table[:, None] * pixels % NPIX
    pixel_angle = pixel_phase.astype(jnp.float32) * (2.0 * math.pi / NPIX)
    weights = jnp.where(order_table == 0, 1.0, 2.0).astype(jnp.float32)[:, None]
    cycle_table = jnp.stack([weights * jnp.cos(pixel_angle), -weights * jnp.sin(pixel_angle)])
    sky_map = jnp.einsum(
        "ksrc,ksj->rjc",
        lax.all_to_all(spectra, "wide", split_axis=2, concat_axis=1, tiled=True),
        cycle_table,
        precision=lax.Precision.HIGHEST,
        preferred_element_type=jnp.float32,
    )
    spectra_rows = lax.all_to_all(sky_map, "narrow", split_axis=1, concat_axis=2, tiled=True)
    cycle_count, pixel_count, chan_count = spectra_rows.shape
    sky_field = spectra_rows.reshape(cycle_count * pixel_count, chan_count)
    lowrank = jnp.zeros_like(sky_field)
    sparse = jnp.zeros_like(sky_field)
    for iteration in range(ITERS):
        sparse = soft_shrink(sky_field - lowrank, thresholds)
        residue = sky_field - sparse
        partial_cov = jnp.dot(
            residue.T, residue, precision=lax.Precision.HIGHEST, preferred_element_type=jnp.float32
        )
        covariance = lax.psum(partial_cov, ("wide", "narrow"))
        lowrank = jnp.dot(
            residue,
            wiener_filter(covariance),
            precision=lax.Precision.HIGHEST,
            preferred_element_type=jnp.float32,
        )
    return (
        lowrank.reshape(cycle_count, pixel_count, chan_count),
        sparse.reshape(cycle_count, pixel_count, chan_count),
    )


def solution(mesh):
    placed = (P(None, "wide", None, "narrow"), P("wide", None, None), P(), P())
    return jax.shard_map(
        per_device,
        mesh=mesh,
        in_specs=placed,
        out_specs=(P("wide", "narrow", None), P("wide", "narrow", None)),
        check_vma=False,
    )
```

profile of v0, /device:TPU:2, one launch (start us, length us, event | category | flops | bytes accessed | tf_op | source)
XLA Modules:
  0.0 966.5 jit_solution(3870654779187750146)
XLA Ops:
  8.0 5.5 fusion.14
  13.5 1.8 copy.24
  15.3 12.0 %all-to-all-start = ((f32[2,16,64,128]{3,0,1,2:T(2,128)}), f32[2,16,64,128]{3,0,1,2:T(2,128)S(1)}, u32[]{:S(2)}, u32[]{:S(2)}) async-start(f32[2,16,64,128]{3,0,1,2:T(2,128)} %copy.24), calls=%async_computation | async-start | bytes 2097152 | tf_op jit(solution)/shard_map/all_to_all | solution.py:41
  27.4 35.0 %cosine_multiply_fusion = (f32[1,1024,2048]{1,2,0:T(8,128)}, f32[1,1024,2048]{1,2,0:T(8,128)}) fusion(s32[1024]{0:T(1024)S(1)} %copy-done.7, f32[1024]{0:T(1024)S(1)} %get-tuple-element.68, f32[1024]{0:T(1024)S(1)} %get-tuple-element.69), kind=kLoop, calls=%fused_computation.17 | loop fusion | flops 33554432 | bytes 16789504 | tf_op jit(solution)/shard_map/mul | solution.py:38
  62.4 16.5 %fusion = f32[2048,128,1]{1,0,2:T(8,128)S(1)} fusion(f32[2,1024,128]{2,1,0:T(8,128)S(1)} %bitcast.179, f32[1,1024,2048]{1,2,0:T(8,128)} %get-tuple-element.67, f32[1,1024,2048]{1,2,0:T(8,128)} %get-tuple-element.66), kind=kOutput, calls=%fused_computation.4 | convolution fusion | flops 6446645248 | bytes 18874368 | tf_op jit(solution)/shard_map/ksrc,ksj->rjc/dot_general | solution.py:39
  79.0 19.9 %all_to_all.30 = f32[1,2048,128]{2,0,1:T(1,128)S(1)} all-to-all(f32[1,2048,128]{2,0,1:T(1,128)S(1)} %bitcast.180), channel_id=1, replica_groups=mesh['wide'=64,'narrow'=4] {'narrow'}, dimensions={1} | all-to-all | bytes 2097152 | tf_op jit(solution)/shard_map/all_to_all | solution.py:46
  99.7 2.8 fusion.143
  102.6 1.4 bitcast_subtract_fusion.1
  104.0 256.8 %all-reduce.4.cloned.1.call-done = f32[512,512]{0,1:T(8,128)} async-done(((f32[512,512]{0,1:T(8,128)}), f32[512,512]{0,1:T(8,128)}) %all-reduce.4.cloned.1.call-update) | async-done | bytes 1048592 | tf_op jit(solution)/shard_map/psum | solution.py:57
  360.7 2.0 select_reduce_fusion.1
  363.4 1.3 select_add_fusion.1
  364.7 1.3 copy.29
  366.0 1.8 fusion.34
  368.8 11.7 %cholesky.286 = f32[128,128]{1,0:T(8,128)S(1)} custom-call(f32[128,128]{1,0:T(8,128)S(1)} %cholesky.426), custom_call_target="Cholesky" | custom-call | tf_op jit(solution)/shard_map/jit(cholesky)/cholesky | solution.py:18
  380.5 9.8 %custom-call.29 = f32[1,128,128]{1,2,0:T(8,128)S(1)} custom-call(f32[1,128,128]{2,1,0:T(8,128)S(1)} %get-tuple-element.65), custom_call_target="InvertDiagBlocksLowerTriangular" | custom-call | tf_op jit(solution)/shard_map/jit(cholesky)/cholesky | solution.py:18
  391.7 1.3 convolution_subtract_fusion.14
  393.0 11.7 %cholesky.305 = f32[128,128]{1,0:T(8,128)S(1)} custom-call(f32[128,128]{1,0:T(8,128)S(1)} %cholesky.430), custom_call_target="Cholesky" | custom-call | tf_op jit(solution)/shard_map/jit(cholesky)/cholesky | solution.py:18
  404.7 18.5 %custom-call.30 = f32[1,128,128]{1,2,0:T(8,128)S(1)} custom-call(f32[1,128,128]{2,1,0:T(8,128)S(1)} %get-tuple-element.62), custom_call_target="InvertDiagBlocksLowerTriangular" | custom-call | tf_op jit(solution)/shard_map/jit(cholesky)/cholesky | solution.py:18
  423.5 1.3 convolution_subtract_fusion.16
  424.8 11.7 %cholesky.326 = f32[128,128]{1,0:T(8,128)S(1)} custom-call(f32[128,128]{1,0:T(8,128)S(1)} %cholesky.435), custom_call_target="Cholesky" | custom-call | tf_op jit(solution)/shard_map/jit(cholesky)/cholesky | solution.py:18
  437.2 9.8 %custom-call.31 = f32[1,128,128]{1,2,0:T(8,128)S(1)} custom-call(f32[1,128,128]{2,1,0:T(8,128)S(1)} %get-tuple-element.59), custom_call_target="InvertDiagBlocksLowerTriangular" | custom-call | tf_op jit(solution)/shard_map/jit(cholesky)/cholesky | solution.py:18
  448.5 12.1 %cholesky.343 = f32[128,128]{1,0:T(8,128)S(1)} custom-call(f32[128,128]{1,0:T(8,128)S(1)} %convolution_subtract_fusion.18), custom_call_target="Cholesky" | custom-call | tf_op jit(solution)/shard_map/jit(cholesky)/cholesky | solution.py:18
  465.6 11.2 %while.4 = (s32[]{:T(128)}, f32[512,512]{1,0:T(8,128)}, s32[4,2]{0,1:T(2,128)S(1)}, f32[4,128,128]{2,1,0:T(8,128)S(1)}, s32[]{:T(128)}) while((s32[]{:T(128)}, f32[512,512]{1,0:T(8,128)}, s32[4,2]{0,1:T(2,128)S(1)}, f32[4,128,128]{2,1,0:T(8,128)S(1)}, s32[]{:T(128)}) %tuple.61), condition=%wide.while_cond, body=%wide.while_body.sunk | while | flops 2 | bytes 131181 | solution.py:21
  466.2 2.2 bitcast_dynamic-update-slice_fusion.4
  469.0 2.2 bitcast_dynamic-update-slice_fusion.4
  471.9 2.2 bitcast_dynamic-update-slice_fusion.4
  474.7 2.1 bitcast_dynamic-update-slice_fusion.4
  477.6 40.1 %custom-call.32 = f32[4,128,128]{1,2,0:T(8,128)S(1)} custom-call(f32[4,128,128]{2,1,0:T(8,128)} %copy-done.5), custom_call_target="InvertDiagBlocksLowerTriangular" | custom-call | tf_op jit(solution)/shard_map/jit(_cho_solve)/triangular_solve | solution.py:21
  518.1 1.4 convolution_subtract_fusion.8
  520.0 1.9 convolution_subtract_fusion.7
  522.3 2.4 convolution_subtract_fusion.12
  525.5 1.3 convolution_subtract_fusion.6
  527.2 1.4 convolution_subtract_fusion.5
  528.9 1.6 convolution_subtract_fusion.11
  530.9 3.3 bitcast_subtract_fusion
  534.2 2.9 fusion.144
  537.1 2.5 copy.39
  539.6 255.4 %all-reduce.6.cloned.1.call-done = f32[512,512]{0,1:T(8,128)} async-done(((f32[512,512]{0,1:T(8,128)}), f32[512,512]{0,1:T(8,128)}) %all-reduce.6.cloned.1.call-update) | async-done | bytes 1048592 | tf_op jit(solution)/shard_map/psum | solution.py:57
  795.1 2.0 select_reduce_fusion
  797.7 1.3 select_add_fusion
  799.0 1.3 copy.35
  800.3 1.8 fusion.33
  803.1 11.9 %cholesky.358 = f32[128,128]{1,0:T(8,128)S(1)} custom-call(f32[128,128]{1,0:T(8,128)S(1)} %cholesky.439), custom_call_target="Cholesky" | custom-call | tf_op jit(solution)/shard_map/jit(cholesky)/cholesky | solution.py:18
  815.1 9.8 %custom-call.33 = f32[1,128,128]{1,2,0:T(8,128)S(1)} custom-call(f32[1,128,128]{2,1,0:T(8,128)S(1)} %get-tuple-element.55), custom_call_target="InvertDiagBlocksLowerTriangular" | custom-call | tf_op jit(solution)/shard_map/jit(cholesky)/cholesky | solution.py:18
  826.2 1.3 convolution_subtract_fusion.13
  827.5 11.7 %cholesky.377 = f32[128,128]{1,0:T(8,128)S(1)} custom-call(f32[128,128]{1,0:T(8,128)S(1)} %cholesky.443), custom_call_target="Cholesky" | custom-call | tf_op jit(solution)/shard_map/jit(cholesky)/cholesky | solution.py:18
  840.6 10.0 %custom-call.34 = f32[1,128,128]{1,2,0:T(8,128)S(1)} custom-call(f32[1,128,128]{2,1,0:T(8,128)S(1)} %get-tuple-element.52), custom_call_target="InvertDiagBlocksLowerTriangular" | custom-call | tf_op jit(solution)/shard_map/jit(cholesky)/cholesky | solution.py:18
  850.8 1.3 convolution_subtract_fusion.15
  852.1 11.7 %cholesky.398 = f32[128,128]{1,0:T(8,128)S(1)} custom-call(f32[128,128]{1,0:T(8,128)S(1)} %cholesky.448), custom_call_target="Cholesky" | custom-call | tf_op jit(solution)/shard_map/jit(cholesky)/cholesky | solution.py:18
  864.5 9.8 %custom-call.35 = f32[1,128,128]{1,2,0:T(8,128)S(1)} custom-call(f32[1,128,128]{2,1,0:T(8,128)S(1)} %get-tuple-element.49), custom_call_target="InvertDiagBlocksLowerTriangular" | custom-call | tf_op jit(solution)/shard_map/jit(cholesky)/cholesky | solution.py:18
  875.8 11.7 %cholesky.415 = f32[128,128]{1,0:T(8,128)S(1)} custom-call(f32[128,128]{1,0:T(8,128)S(1)} %convolution_subtract_fusion.17), custom_call_target="Cholesky" | custom-call | tf_op jit(solution)/shard_map/jit(cholesky)/cholesky | solution.py:18
  891.8 11.7 %while.5 = (s32[]{:T(128)}, f32[512,512]{1,0:T(8,128)}, s32[4,2]{0,1:T(2,128)S(1)}, f32[4,128,128]{2,1,0:T(8,128)S(1)}, s32[]{:T(128)}) while((s32[]{:T(128)}, f32[512,512]{1,0:T(8,128)}, s32[4,2]{0,1:T(2,128)S(1)}, f32[4,128,128]{2,1,0:T(8,128)S(1)}, s32[]{:T(128)}) %tuple.71), condition=%wide.while_cond.clone, body=%wide.while_body.clone.sunk | while | flops 2 | bytes 131181 | solution.py:21
  892.5 2.3 bitcast_dynamic-update-slice_fusion.5
  895.5 2.3 bitcast_dynamic-update-slice_fusion.5
  898.4 2.3 bitcast_dynamic-update-slice_fusion.5
  901.4 2.2 bitcast_dynamic-update-slice_fusion.5
  903.6 39.6 %custom-call.36 = f32[4,128,128]{1,2,0:T(8,128)S(1)} custom-call(f32[4,128,128]{2,1,0:T(8,128)S(1)} %get-tuple-element.19), custom_call_target="InvertDiagBlocksLowerTriangular" | custom-call | tf_op jit(solution)/shard_map/jit(_cho_solve)/triangular_solve | solution.py:21
  943.6 1.4 convolution_subtract_fusion.4
  945.4 1.9 convolution_subtract_fusion.3
  947.8 2.4 convolution_subtract_fusion.10
  951.0 1.3 convolution_subtract_fusion.2
  952.6 1.4 convolution_subtract_fusion.1
  954.4 1.6 convolution_subtract_fusion.9
  956.3 2.8 convolution_bitcast_fusion
  (96 shorter events, 29.3 us)
Async XLA Ops:
  8.0 19.3 %copy-start.7 = (s32[1024]{0:T(1024)S(1)}, s32[1024]{0:T(1024)}, u32[]{:S(2)}) copy-start(s32[1024]{0:T(1024)} %param.9) | copy-start | bytes 12292
  15.3 47.1 %all-to-all-start = ((f32[2,16,64,128]{3,0,1,2:T(2,128)}), f32[2,16,64,128]{3,0,1,2:T(2,128)S(1)}, u32[]{:S(2)}, u32[]{:S(2)}) async-start(f32[2,16,64,128]{3,0,1,2:T(2,128)} %copy.24), calls=%async_computation | async-start | bytes 2097152 | tf_op jit(solution)/shard_map/all_to_all | solution.py:41
  27.3 333.4 %all-reduce.4.cloned.1.call-start = ((), (), s32[]{:S(2)}) async-start(), calls=%async_computation.2 | async-start | bytes 2097152 | tf_op jit(solution)/shard_map/psum | solution.py:57
  62.4 36.8 %copy-start.6 = (f32[512]{0:T(512)S(1)}, f32[512]{0:T(512)}, u32[]{:S(2)}) copy-start(f32[512]{0:T(512)} %param.10) | copy-start | bytes 6148
  102.5 692.5 %all-reduce.6.cloned.1.call-start = ((), (), s32[]{:S(2)}) async-start(), calls=%async_computation.3 | async-start | bytes 2097152 | tf_op jit(solution)/shard_map/psum | solution.py:57
  360.7 157.0 %copy-start = (f32[512,512]{0,1:T(8,128)S(1)}, f32[512,512]{0,1:T(8,128)}, u32[]{:S(2)}) copy-start(f32[512,512]{0,1:T(8,128)} %all-reduce.4.cloned.1.call-done) | copy-start | bytes 3145732
  367.8 1.0 copy-start.4
  465.6 65.4 %copy-start.2 = (f32[512,512]{0,1:T(8,128)S(1)}, f32[512,512]{0,1:T(8,128)}, u32[]{:S(2)}) copy-start(f32[512,512]{0,1:T(8,128)} %bitcast_subtract_fusion.1) | copy-start | bytes 3145732
  476.8 0.7 copy-start.5
  795.1 148.1 %copy-start.1 = (f32[512,512]{0,1:T(8,128)S(1)}, f32[512,512]{0,1:T(8,128)}, u32[]{:S(2)}) copy-start(f32[512,512]{0,1:T(8,128)} %all-reduce.6.cloned.1.call-done) | copy-start | bytes 3145732
  802.1 1.0 copy-start.3
Sparse Core Ops, SparseCore 0:
  102.6 258.0 all-reduce.3
  537.2 257.7 all-reduce.5
where the time goes:
time: 975 us; the launch traced here: 966 us
  waiting for transfers between devices  512 us (53%)
  other arithmetic  296 us (30%)
  matrix products  71 us (7%)
  local copies, waits for them, and re-layouts  33.9 us (3%)
  between operations  21.4 us (2%)
  blocking collectives  19.9 us (2%)
  starting transfers between devices  12.1 us (1%)
    psum x2, waiting for transfers between devices, per_device(): covariance = lax.psum(partial_cov, ('wide', 'narrow'))  512 us
    another operation x29, other arithmetic, wiener_filter(): jnp.linalg.cholesky(covariance + ridge_shift * jnp.eye(chan_total, dtype=...  167 us
    another operation x5, other arithmetic, wiener_filter(): return jax.scipy.linalg.cho_solve((factor, True), covariance)  81.9 us
    mul x1, other arithmetic, per_device(): weights * jnp.cos(pixel_angle)  35 us
    another operation x28, matrix products, wiener_filter(): return jax.scipy.linalg.cho_solve((factor, True), covariance)  26.2 us
    another operation x27, local copies, waits for them, and re-layouts, wiener_filter(): return jax.scipy.linalg.cho_solve((factor, True), covariance)  22.8 us
    all_to_all x1, blocking collectives, per_device(): lax.all_to_all(sky_map, 'narrow', split_axis=1, concat_axis=2, tiled=True)  19.9 us
  transfers between devices with their start and end apart: 3, of which 2 were waited for; matrix products, arithmetic and copies ran while one was open for 4% of the time, Pallas kernels for 0%

commit v1 on v0

--- a/solution.py
+++ b/solution.py
@@ -54,7 +54,7 @@
         partial_cov = jnp.dot(
             residue.T, residue, precision=lax.Precision.HIGHEST, preferred_element_type=jnp.float32
         )
-        covariance = lax.psum(partial_cov, ("wide", "narrow"))
+        covariance = lax.psum(lax.psum(partial_cov, "wide"), "narrow")
         lowrank = jnp.dot(
             residue,
             wiener_filter(covariance),

time: 975 us -> 935 us (0.959)
  waiting for transfers between devices: 512 us -> 472 us
    psum x2 -> x4, waiting for transfers between devices: 512 us -> 472 us  [per_device(): covariance = lax.psum(lax.psum(partial_cov, 'wide'), 'narrow')]
  transfers between devices with their start and end apart: 3 -> 5, of which waited for: 2 -> 4; matrix products, arithmetic and copies ran while one was open for 4% -> 4% of each run, Pallas kernels for 0% -> 0%
where the time goes in v1:
time: 935 us; the launch traced here: 926 us
  waiting for transfers between devices  472 us (50%)
  other arithmetic  296 us (32%)
  matrix products  70.9 us (8%)
  local copies, waits for them, and re-layouts  34.3 us (4%)
  between operations  21.2 us (2%)
  blocking collectives  19.9 us (2%)
  starting transfers between devices  12.3 us (1%)
    psum x4, waiting for transfers between devices, per_device(): covariance = lax.psum(lax.psum(partial_cov, 'wide'), 'narrow')  472 us
    another operation x29, other arithmetic, wiener_filter(): jnp.linalg.cholesky(covariance + ridge_shift * jnp.eye(chan_total, dtype=...  167 us
    another operation x5, other arithmetic, wiener_filter(): return jax.scipy.linalg.cho_solve((factor, True), covariance)  81.6 us
    mul x1, other arithmetic, per_device(): weights * jnp.cos(pixel_angle)  35 us
    another operation x28, matrix products, wiener_filter(): return jax.scipy.linalg.cho_solve((factor, True), covariance)  26.2 us
    another operation x27, local copies, waits for them, and re-layouts, wiener_filter(): return jax.scipy.linalg.cho_solve((factor, True), covariance)  23.3 us
    all_to_all x1, blocking collectives, per_device(): lax.all_to_all(sky_map, 'narrow', split_axis=1, concat_axis=2, tiled=True)  19.9 us
  transfers between devices with their start and end apart: 5, of which 4 were waited for; matrix products, arithmetic and copies ran while one was open for 4% of the time, Pallas kernels for 0%

profile of v1, /device:TPU:2, one launch (start us, length us, event | category | flops | bytes accessed | tf_op | source)
XLA Modules:
  0.0 926.3 jit_solution(7749570123790843614)
XLA Ops:
  8.0 5.5 fusion.14
  13.5 1.8 copy.24
  15.3 12.0 %all-to-all-start = ((f32[2,16,64,128]{3,0,1,2:T(2,128)}), f32[2,16,64,128]{3,0,1,2:T(2,128)S(1)}, u32[]{:S(2)}, u32[]{:S(2)}) async-start(f32[2,16,64,128]{3,0,1,2:T(2,128)} %copy.24), calls=%async_computation | async-start | bytes 2097152 | tf_op jit(solution)/shard_map/all_to_all | solution.py:41
  27.4 35.0 %cosine_multiply_fusion = (f32[1,1024,2048]{1,2,0:T(8,128)}, f32[1,1024,2048]{1,2,0:T(8,128)}) fusion(s32[1024]{0:T(1024)S(1)} %copy-done.7, f32[1024]{0:T(1024)S(1)} %get-tuple-element.68, f32[1024]{0:T(1024)S(1)} %get-tuple-element.69), kind=kLoop, calls=%fused_computation.17 | loop fusion | flops 33554432 | bytes 16789504 | tf_op jit(solution)/shard_map/mul | solution.py:38
  62.4 16.5 %fusion = f32[2048,128,1]{1,0,2:T(8,128)S(1)} fusion(f32[2,1024,128]{2,1,0:T(8,128)S(1)} %bitcast.179, f32[1,1024,2048]{1,2,0:T(8,128)} %get-tuple-element.67, f32[1,1024,2048]{1,2,0:T(8,128)} %get-tuple-element.66), kind=kOutput, calls=%fused_computation.4 | convolution fusion | flops 6446645248 | bytes 18874368 | tf_op jit(solution)/shard_map/ksrc,ksj->rjc/dot_general | solution.py:39
  79.0 19.9 %all_to_all.30 = f32[1,2048,128]{2,0,1:T(1,128)S(1)} all-to-all(f32[1,2048,128]{2,0,1:T(1,128)S(1)} %bitcast.180), channel_id=1, replica_groups=mesh['wide'=64,'narrow'=4] {'narrow'}, dimensions={1} | all-to-all | bytes 2097152 | tf_op jit(solution)/shard_map/all_to_all | solution.py:46
  99.7 2.8 fusion.143
  102.6 186.3 %all-reduce.6.cloned.1.call-done = f32[512,512]{0,1:T(8,128)} async-done(((f32[512,512]{0,1:T(8,128)}), f32[512,512]{0,1:T(8,128)}) %all-reduce.6.cloned.1.call-update) | async-done | bytes 1048592 | tf_op jit(solution)/shard_map/psum | solution.py:57
  288.9 1.4 bitcast_subtract_fusion.1
  290.3 49.4 %all-reduce.8.cloned.1.call-done = f32[512,512]{0,1:T(8,128)} async-done(((f32[512,512]{0,1:T(8,128)}), f32[512,512]{0,1:T(8,128)}) %all-reduce.8.cloned.1.call-update) | async-done | bytes 1048592 | tf_op jit(solution)/shard_map/psum | solution.py:57
  339.7 2.0 select_reduce_fusion.1
  342.3 1.3 select_add_fusion.1
  343.7 1.3 copy.29
  345.0 1.8 fusion.34
  347.7 11.7 %cholesky.286 = f32[128,128]{1,0:T(8,128)S(1)} custom-call(f32[128,128]{1,0:T(8,128)S(1)} %cholesky.426), custom_call_target="Cholesky" | custom-call | tf_op jit(solution)/shard_map/jit(cholesky)/cholesky | solution.py:18
  359.5 9.8 %custom-call.29 = f32[1,128,128]{1,2,0:T(8,128)S(1)} custom-call(f32[1,128,128]{2,1,0:T(8,128)S(1)} %get-tuple-element.65), custom_call_target="InvertDiagBlocksLowerTriangular" | custom-call | tf_op jit(solution)/shard_map/jit(cholesky)/cholesky | solution.py:18
  371.9 11.7 %cholesky.305 = f32[128,128]{1,0:T(8,128)S(1)} custom-call(f32[128,128]{1,0:T(8,128)S(1)} %cholesky.430), custom_call_target="Cholesky" | custom-call | tf_op jit(solution)/shard_map/jit(cholesky)/cholesky | solution.py:18
  383.7 18.5 %custom-call.30 = f32[1,128,128]{1,2,0:T(8,128)S(1)} custom-call(f32[1,128,128]{2,1,0:T(8,128)S(1)} %get-tuple-element.62), custom_call_target="InvertDiagBlocksLowerTriangular" | custom-call | tf_op jit(solution)/shard_map/jit(cholesky)/cholesky | solution.py:18
  402.5 1.3 convolution_subtract_fusion.16
  403.8 11.7 %cholesky.326 = f32[128,128]{1,0:T(8,128)S(1)} custom-call(f32[128,128]{1,0:T(8,128)S(1)} %cholesky.435), custom_call_target="Cholesky" | custom-call | tf_op jit(solution)/shard_map/jit(cholesky)/cholesky | solution.py:18
  416.2 9.8 %custom-call.31 = f32[1,128,128]{1,2,0:T(8,128)S(1)} custom-call(f32[1,128,128]{2,1,0:T(8,128)S(1)} %get-tuple-element.59), custom_call_target="InvertDiagBlocksLowerTriangular" | custom-call | tf_op jit(solution)/shard_map/jit(cholesky)/cholesky | solution.py:18
  427.5 12.1 %cholesky.343 = f32[128,128]{1,0:T(8,128)S(1)} custom-call(f32[128,128]{1,0:T(8,128)S(1)} %convolution_subtract_fusion.18), custom_call_target="Cholesky" | custom-call | tf_op jit(solution)/shard_map/jit(cholesky)/cholesky | solution.py:18
  444.6 11.7 %while.4 = (s32[]{:T(128)}, f32[512,512]{1,0:T(8,128)}, s32[4,2]{0,1:T(2,128)S(1)}, f32[4,128,128]{2,1,0:T(8,128)S(1)}, s32[]{:T(128)}) while((s32[]{:T(128)}, f32[512,512]{1,0:T(8,128)}, s32[4,2]{0,1:T(2,128)S(1)}, f32[4,128,128]{2,1,0:T(8,128)S(1)}, s32[]{:T(128)}) %tuple.61), condition=%wide.while_cond, body=%wide.while_body.sunk | while | flops 2 | bytes 131181 | solution.py:21
  445.3 2.3 bitcast_dynamic-update-slice_fusion.4
  448.2 2.3 bitcast_dynamic-update-slice_fusion.4
  451.2 2.3 bitcast_dynamic-update-slice_fusion.4
  454.1 2.2 bitcast_dynamic-update-slice_fusion.4
  457.0 40.1 %custom-call.32 = f32[4,128,128]{1,2,0:T(8,128)S(1)} custom-call(f32[4,128,128]{2,1,0:T(8,128)} %copy-done.5), custom_call_target="InvertDiagBlocksLowerTriangular" | custom-call | tf_op jit(solution)/shard_map/jit(_cho_solve)/triangular_solve | solution.py:21
  497.6 1.4 convolution_subtract_fusion.8
  499.5 1.9 convolution_subtract_fusion.7
  501.8 2.4 convolution_subtract_fusion.12
  505.0 1.3 convolution_subtract_fusion.6
  506.7 1.4 convolution_subtract_fusion.5
  508.4 1.6 convolution_subtract_fusion.11
  510.4 3.3 bitcast_subtract_fusion
  513.6 2.8 fusion.144
  516.7 187.9 %all-reduce.10.cloned.1.call-done = f32[512,512]{0,1:T(8,128)} async-done(((f32[512,512]{0,1:T(8,128)}), f32[512,512]{0,1:T(8,128)}) %all-reduce.10.cloned.1.call-update) | async-done | bytes 1048592 | tf_op jit(solution)/shard_map/psum | solution.py:57
  704.7 2.5 copy.39
  707.2 48.1 %all-reduce.12.cloned.1.call-done = f32[512,512]{0,1:T(8,128)} async-done(((f32[512,512]{0,1:T(8,128)}), f32[512,512]{0,1:T(8,128)}) %all-reduce.12.cloned.1.call-update) | async-done | bytes 1048592 | tf_op jit(solution)/shard_map/psum | solution.py:57
  755.3 2.0 select_reduce_fusion
  758.0 1.3 select_add_fusion
  759.3 1.3 copy.35
  760.6 1.8 fusion.33
  763.4 11.7 %cholesky.358 = f32[128,128]{1,0:T(8,128)S(1)} custom-call(f32[128,128]{1,0:T(8,128)S(1)} %cholesky.439), custom_call_target="Cholesky" | custom-call | tf_op jit(solution)/shard_map/jit(cholesky)/cholesky | solution.py:18
  775.3 9.8 %custom-call.33 = f32[1,128,128]{1,2,0:T(8,128)S(1)} custom-call(f32[1,128,128]{2,1,0:T(8,128)S(1)} %get-tuple-element.55), custom_call_target="InvertDiagBlocksLowerTriangular" | custom-call | tf_op jit(solution)/shard_map/jit(cholesky)/cholesky | solution.py:18
  787.6 11.7 %cholesky.377 = f32[128,128]{1,0:T(8,128)S(1)} custom-call(f32[128,128]{1,0:T(8,128)S(1)} %cholesky.443), custom_call_target="Cholesky" | custom-call | tf_op jit(solution)/shard_map/jit(cholesky)/cholesky | solution.py:18
  800.7 10.0 %custom-call.34 = f32[1,128,128]{1,2,0:T(8,128)S(1)} custom-call(f32[1,128,128]{2,1,0:T(8,128)S(1)} %get-tuple-element.52), custom_call_target="InvertDiagBlocksLowerTriangular" | custom-call | tf_op jit(solution)/shard_map/jit(cholesky)/cholesky | solution.py:18
  811.0 1.3 convolution_subtract_fusion.15
  812.3 11.7 %cholesky.398 = f32[128,128]{1,0:T(8,128)S(1)} custom-call(f32[128,128]{1,0:T(8,128)S(1)} %cholesky.448), custom_call_target="Cholesky" | custom-call | tf_op jit(solution)/shard_map/jit(cholesky)/cholesky | solution.py:18
  824.7 9.8 %custom-call.35 = f32[1,128,128]{1,2,0:T(8,128)S(1)} custom-call(f32[1,128,128]{2,1,0:T(8,128)S(1)} %get-tuple-element.49), custom_call_target="InvertDiagBlocksLowerTriangular" | custom-call | tf_op jit(solution)/shard_map/jit(cholesky)/cholesky | solution.py:18
  835.9 11.9 %cholesky.415 = f32[128,128]{1,0:T(8,128)S(1)} custom-call(f32[128,128]{1,0:T(8,128)S(1)} %convolution_subtract_fusion.17), custom_call_target="Cholesky" | custom-call | tf_op jit(solution)/shard_map/jit(cholesky)/cholesky | solution.py:18
  852.2 11.7 %while.5 = (s32[]{:T(128)}, f32[512,512]{1,0:T(8,128)}, s32[4,2]{0,1:T(2,128)S(1)}, f32[4,128,128]{2,1,0:T(8,128)S(1)}, s32[]{:T(128)}) while((s32[]{:T(128)}, f32[512,512]{1,0:T(8,128)}, s32[4,2]{0,1:T(2,128)S(1)}, f32[4,128,128]{2,1,0:T(8,128)S(1)}, s32[]{:T(128)}) %tuple.75), condition=%wide.while_cond.clone, body=%wide.while_body.clone.sunk | while | flops 2 | bytes 131181 | solution.py:21
  852.9 2.3 bitcast_dynamic-update-slice_fusion.5
  855.8 2.3 bitcast_dynamic-update-slice_fusion.5
  858.8 2.3 bitcast_dynamic-update-slice_fusion.5
  861.7 2.2 bitcast_dynamic-update-slice_fusion.5
  863.9 39.3 %custom-call.36 = f32[4,128,128]{1,2,0:T(8,128)S(1)} custom-call(f32[4,128,128]{2,1,0:T(8,128)S(1)} %get-tuple-element.19), custom_call_target="InvertDiagBlocksLowerTriangular" | custom-call | tf_op jit(solution)/shard_map/jit(_cho_solve)/triangular_solve | solution.py:21
  903.7 1.4 convolution_subtract_fusion.4
  905.6 1.9 convolution_subtract_fusion.3
  907.9 2.4 convolution_subtract_fusion.10
  911.1 1.3 convolution_subtract_fusion.2
  912.7 1.4 convolution_subtract_fusion.1
  914.5 1.6 convolution_subtract_fusion.9
  916.5 2.8 convolution_bitcast_fusion
  (102 shorter events, 32.3 us)
Async XLA Ops:
  8.0 19.3 %copy-start.7 = (s32[1024]{0:T(1024)S(1)}, s32[1024]{0:T(1024)}, u32[]{:S(2)}) copy-start(s32[1024]{0:T(1024)} %param.9) | copy-start | bytes 12292
  15.3 47.1 %all-to-all-start = ((f32[2,16,64,128]{3,0,1,2:T(2,128)}), f32[2,16,64,128]{3,0,1,2:T(2,128)S(1)}, u32[]{:S(2)}, u32[]{:S(2)}) async-start(f32[2,16,64,128]{3,0,1,2:T(2,128)} %copy.24), calls=%async_computation | async-start | bytes 2097152 | tf_op jit(solution)/shard_map/all_to_all | solution.py:41
  27.3 261.6 %all-reduce.6.cloned.1.call-start = ((), (), s32[]{:S(2)}) async-start(), calls=%async_computation.2 | async-start | bytes 2097152 | tf_op jit(solution)/shard_map/psum | solution.py:57
  62.4 36.8 %copy-start.6 = (f32[512]{0:T(512)S(1)}, f32[512]{0:T(512)}, u32[]{:S(2)}) copy-start(f32[512]{0:T(512)} %param.10) | copy-start | bytes 6148
  102.5 237.2 %all-reduce.8.cloned.1.call-start = ((), (), s32[]{:S(2)}) async-start(), calls=%async_computation.3 | async-start | bytes 2097152 | tf_op jit(solution)/shard_map/psum | solution.py:57
  288.9 415.8 %all-reduce.10.cloned.1.call-start = ((), (), s32[]{:S(2)}) async-start(), calls=%async_computation.4 | async-start | bytes 2097152 | tf_op jit(solution)/shard_map/psum | solution.py:57
  339.7 157.5 %copy-start = (f32[512,512]{0,1:T(8,128)S(1)}, f32[512,512]{0,1:T(8,128)}, u32[]{:S(2)}) copy-start(f32[512,512]{0,1:T(8,128)} %all-reduce.8.cloned.1.call-done) | copy-start | bytes 3145732
  346.7 1.0 copy-start.4
  444.6 65.8 %copy-start.2 = (f32[512,512]{0,1:T(8,128)S(1)}, f32[512,512]{0,1:T(8,128)}, u32[]{:S(2)}) copy-start(f32[512,512]{0,1:T(8,128)} %bitcast_subtract_fusion.1) | copy-start | bytes 3145732
  456.3 0.7 copy-start.5
  516.5 238.8 %all-reduce.12.cloned.1.call-start = ((), (), s32[]{:S(2)}) async-start(), calls=%async_computation.5 | async-start | bytes 2097152 | tf_op jit(solution)/shard_map/psum | solution.py:57
  755.3 147.9 %copy-start.1 = (f32[512,512]{0,1:T(8,128)S(1)}, f32[512,512]{0,1:T(8,128)}, u32[]{:S(2)}) copy-start(f32[512,512]{0,1:T(8,128)} %all-reduce.12.cloned.1.call-done) | copy-start | bytes 3145732
  762.4 1.0 copy-start.3
Sparse Core Ops, SparseCore 0:
  102.6 186.1 all-reduce.5
  291.2 48.4 all-reduce.7
  516.6 187.9 all-reduce.9
  706.9 48.4 all-reduce.11
